TPU v7x, 128 devices: a whole 4x4x4 slice. The times are simulated.
128 devices in a mesh: atom: 32 (over z, y, core), dp: 4 (over x).
Axes of the slice: x: 4, y: 4, z: 4, core: 2. Of those that a mesh axis runs over, the one named last changes fastest.
Arguments:
- activations: bfloat16 [512, 8192], P('dp'), may hold values from -6 to 6
- dictionary: bfloat16 [8192, 65536], P('dp', 'atom'), may hold values from -0.03535534 to 0.03535534
Outputs:
- sparse_codes: float32 [512, 65536], P('dp', 'atom')
- residual: float32 [512, 8192], P('atom', 'dp')
- new_dictionary: bfloat16 [8192, 65536], P('dp', 'atom')
All inputs are finite; a program needn't handle non-finite values.
Results may differ from a plain program's by a relative error of at most 0.0025.
Values may be sent and summed in bfloat16 or wider, within the bound.
No kernel may reach another device: no remote copies, remote signals or barrier semaphores. Data moves between devices by JAX's collectives and lax.ppermute only.
A program may use at most 128 MiB of HBM per device.

v0:
```python
import jax
import jax.numpy as jnp
from jax import lax
from jax.sharding import PartitionSpec as P

D = 8192
ITERS = 2
threshold = 0.05
step_size = 2.0
learn_rate = 1.0 / 16384.0
epsilon = 1e-12


def shrink(values):
    return values - jnp.clip(values, -threshold, threshold)


def product(left, right):
    return jnp.dot(
        left.astype(jnp.float32),
        right,
        precision=lax.Precision.HIGHEST,
        preferred_element_type=jnp.float32,
    )


def body(activations, dictionary):
    row_count = activations.shape[0]
    dict_wide = dictionary.astype(jnp.float32)
    feature_block = lax.all_to_all(activations, "dp", split_axis=1, concat_axis=0, tiled=True)
    inputs = feature_block.astype(jnp.float32)
    share_rows = feature_block.shape[0] // lax.axis_size("atom")
    offset = lax.axis_index("atom") * share_rows

    def residual_of(coded_rows):
        recon_part = product(coded_rows, dict_wide.T)
        summed = lax.psum(recon_part, "atom")
        full_residual = inputs - summed
        rounded = full_residual.astype(jnp.bfloat16)
        own_residual = lax.dynamic_slice_in_dim(full_residual, offset, share_rows, 0)
        return (rounded, own_residual)

    sparse_codes = jnp.zeros((row_count, dictionary.shape[1]), jnp.float32)
    rounded = feature_block
    coded_rows = None
    residual = None
    for iteration in range(ITERS):
        if iteration > 0:
            rounded, residual = residual_of(coded_rows)

        def encode_rows(first_row, row_total, source=rounded):
            return product(source, dict_wide)

        drive_term = lax.psum_scatter(
            encode_rows(jnp.int32(0), lax.axis_size("dp") * row_count),
            "dp",
            scatter_dimension=0,
            tiled=True,
        )
        sparse_codes = shrink(sparse_codes + step_size * drive_term)
        coded_rows = lax.all_gather(sparse_codes.astype(jnp.bfloat16), "dp", axis=0, tiled=True)
    rounded, residual = residual_of(coded_rows)
    gradient = product(rounded.T, coded_rows.astype(jnp.float32))
    updated = dict_wide + learn_rate * gradient
    squares = lax.psum(jnp.sum(updated * updated, axis=0), "dp")
    new_dictionary = (updated * lax.rsqrt(squares / D + epsilon)).astype(jnp.bfloat16)
    return (sparse_codes, residual, new_dictionary)


def solution(mesh):
    placed = (P("dp", None), P("dp", "atom"))
    return jax.shard_map(
        body,
        mesh=mesh,
        in_specs=placed,
        out_specs=(P("dp", "atom"), P("atom", "dp"), P("dp", "atom")),
        check_vma=False,
    )
```

profile of v0, /device:TPU:24, one launch (start us, length us, event | category | flops | bytes accessed | tf_op | source)
XLA Modules:
  0.0 507.2 jit_solution(12741930514416772770)
XLA Ops:
  7.2 0.0 reduce-scatter.3.cloned.1.call-start
  7.2 0.0 copy-start
  7.2 1.9 copy.8
  9.1 30.7 %all_to_all.19 = bf16[128,4,2048]{2,0,1:T(8,128)(2,1)S(1)} all-to-all(bf16[128,4,2048]{2,0,1:T(8,128)(2,1)S(1)} %bitcast.18), channel_id=1, replica_groups=mesh['atom'=32,'dp'=4] {'dp'}, dimensions={1} | all-to-all | bytes 4194304 | tf_op jit(solution)/shard_map/all_to_all | solution.py:30
  39.8 0.0 copy-done
  39.8 6.0 %fusion.7 = f32[512,2048]{1,0:T(8,128)} fusion(bf16[512,2048]{1,0:T(8,128)(2,1)S(1)} %bitcast.16, bf16[2048,2048]{1,0:T(8,128)(2,1)S(1)} %copy-done), kind=kOutput, calls=%fused_computation.16 | convolution fusion | flops 4294967296 | bytes 14680064 | tf_op jit(solution)/shard_map/dot_general | solution.py:19
  45.8 0.0 reduce-scatter.3.cloned.1.call-update
  45.8 0.0 all-gather.3.cloned.1.call-start
  45.9 47.2 %reduce-scatter.3.cloned.1.call-done = f32[128,2048]{1,0:T(8,128)} async-done(((f32[512,2048]{1,0:T(8,128)}), f32[128,2048]{1,0:T(8,128)}) %reduce-scatter.3.cloned.1.call-update) | async-done | bytes 1048592 | tf_op jit(solution)/shard_map/reduce_scatter | solution.py:54
  93.0 2.2 fusion.5
  95.2 0.0 all-gather.3.cloned.1.call-update
  95.2 0.0 all-reduce.3.cloned.1.call-start
  95.3 30.6 %all-gather.3.cloned.1.call-done = bf16[512,2048]{1,0:T(8,128)(2,1)} async-done(((bf16[128,2048]{1,0:T(8,128)(2,1)}), bf16[512,2048]{1,0:T(8,128)(2,1)}) %all-gather.3.cloned.1.call-update) | async-done | bytes 2097168 | tf_op jit(solution)/shard_map/all_gather | solution.py:61
  125.8 10.6 %fusion.8 = f32[512,2048]{1,0:T(8,128)} fusion(bf16[512,2048]{1,0:T(8,128)(2,1)} %all-gather.3.cloned.1.call-done, bf16[2048,2048]{1,0:T(8,128)(2,1)} %param.3), kind=kOutput, calls=%fused_computation.17 | convolution fusion | flops 4294967296 | bytes 14680064 | tf_op jit(solution)/shard_map/dot_general | solution.py:19
  136.4 0.0 all-reduce.3.cloned.1.call-update
  136.4 0.0 reduce-scatter.5.cloned.1.call-start
  136.5 112.7 %all-reduce.3.cloned.1.call-done = f32[512,2048]{1,0:T(8,128)} async-done(((f32[512,2048]{1,0:T(8,128)}), f32[512,2048]{1,0:T(8,128)}) %all-reduce.3.cloned.1.call-update) | async-done | bytes 4194320 | tf_op jit(solution)/shard_map/psum | solution.py:37
  249.2 11.2 %fusion.1 = f32[512,2048]{1,0:T(8,128)} fusion(bf16[2048,2048]{1,0:T(8,128)(2,1)} %param.3, f32[512,2048]{1,0:T(8,128)} %all-reduce.3.cloned.1.call-done, bf16[512,2048]{1,0:T(8,128)(2,1)S(1)} %bitcast.17), kind=kOutput, calls=%fused_computation.6 | convolution fusion | flops 4298113024 | bytes 18874368 | tf_op jit(solution)/shard_map/dot_general | solution.py:19
  260.4 0.0 copy-start.1
  260.4 0.0 reduce-scatter.5.cloned.1.call-update
  260.4 0.0 all-gather.5.cloned.1.call-start
  260.4 45.7 %reduce-scatter.5.cloned.1.call-done = f32[128,2048]{1,0:T(8,128)} async-done(((f32[512,2048]{1,0:T(8,128)}), f32[128,2048]{1,0:T(8,128)}) %reduce-scatter.5.cloned.1.call-update) | async-done | bytes 1048592 | tf_op jit(solution)/shard_map/reduce_scatter | solution.py:54
  306.1 0.0 copy-done.1
  306.1 2.6 fusion.6
  308.8 0.0 all-gather.5.cloned.1.call-update
  308.8 0.2 all-reduce.5.cloned.1.call-start
  309.0 30.4 %all-gather.5.cloned.1.call-done = bf16[512,2048]{1,0:T(8,128)(2,1)} async-done(((bf16[128,2048]{1,0:T(8,128)(2,1)}), bf16[512,2048]{1,0:T(8,128)(2,1)}) %all-gather.5.cloned.1.call-update) | async-done | bytes 2097168 | tf_op jit(solution)/shard_map/all_gather | solution.py:61
  339.4 10.6 %fusion.9 = f32[512,2048]{1,0:T(8,128)} fusion(bf16[512,2048]{1,0:T(8,128)(2,1)} %all-gather.5.cloned.1.call-done, bf16[2048,2048]{1,0:T(8,128)(2,1)} %param.3), kind=kOutput, calls=%fused_computation.18 | convolution fusion | flops 4294967296 | bytes 14680064 | tf_op jit(solution)/shard_map/dot_general | solution.py:19
  350.0 0.0 all-reduce.5.cloned.1.call-update
  350.0 112.7 %all-reduce.5.cloned.1.call-done = f32[512,2048]{1,0:T(8,128)} async-done(((f32[512,2048]{1,0:T(8,128)}), f32[512,2048]{1,0:T(8,128)}) %all-reduce.5.cloned.1.call-update) | async-done | bytes 4194320 | tf_op jit(solution)/shard_map/psum | solution.py:37
  462.7 0.0 copy-start.2
  462.7 2.9 convert_subtract_fusion
  465.7 0.7 constant_dynamic-slice_fusion
  466.3 0.0 copy-done.2
  466.3 11.3 %multiply_reduce_fusion = (f32[2048]{0:T(1024)S(1)}, f32[2048,2048]{1,0:T(8,128)}) fusion(bf16[2048,2048]{1,0:T(8,128)(2,1)} %param.3, bf16[512,2048]{1,0:T(8,128)(2,1)S(1)} %copy-done.2, f32[512,2048]{1,0:T(8,128)S(1)} %convert_subtract_fusion), kind=kOutput, calls=%fused_computation.1 | convolution fusion | flops 4316985344 | bytes 31465472 | tf_op jit(solution)/shard_map/dot_general | solution.py:19
  477.7 10.5 %psum.23 = f32[2048]{0:T(1024)S(1)} all-reduce(f32[2048]{0:T(1024)S(1)} %get-tuple-element.5), channel_id=1, replica_groups=mesh['atom'=32,'dp'=4] {'dp'}, use_global_device_ids=true, to_apply=%region_5.6 | all-reduce | flops 2048 | bytes 16384 | tf_op jit(solution)/shard_map/psum | solution.py:65
  488.2 12.1 %multiply_convert_fusion = bf16[2048,2048]{1,0:T(8,128)(2,1)} fusion(f32[2048,2048]{1,0:T(8,128)} %get-tuple-element.6, bf16[2048,2048]{1,0:T(8,128)(2,1)} %param.3, f32[2048]{0:T(1024)S(1)} %add_rsqrt_fusion), kind=kLoop, calls=%fused_computation | loop fusion | flops 20971520 | bytes 33562624 | tf_op jit(solution)/shard_map/convert_element_type | solution.py:66
  (1 shorter events, 0.0 us)
Async XLA Ops:
  7.2 85.9 %reduce-scatter.3.cloned.1.call-start = ((), (), s32[]{:S(2)}) async-start(), calls=%async_computation.3 | async-start | bytes 5242880 | tf_op jit(solution)/shard_map/reduce_scatter | solution.py:54
  7.2 32.6 %copy-start = (bf16[2048,2048]{1,0:T(8,128)(2,1)S(1)}, bf16[2048,2048]{1,0:T(8,128)(2,1)}, u32[]{:S(2)}) copy-start(bf16[2048,2048]{1,0:T(8,128)(2,1)} %param.3) | copy-start | bytes 25165828
  45.8 80.0 %all-gather.3.cloned.1.call-start = ((), (), s32[]{:S(2)}) async-start(), calls=%async_computation.4 | async-start | bytes 2621440 | tf_op jit(solution)/shard_map/all_gather | solution.py:61
  95.2 154.0 %all-reduce.3.cloned.1.call-start = ((), (), s32[]{:S(2)}) async-start(), calls=%async_computation.5 | async-start | bytes 8388608 | tf_op jit(solution)/shard_map/psum | solution.py:37
  136.4 169.7 %reduce-scatter.5.cloned.1.call-start = ((), (), s32[]{:S(2)}) async-start(), calls=%async_computation.6 | async-start | bytes 5242880 | tf_op jit(solution)/shard_map/reduce_scatter | solution.py:54
  260.4 45.8 %copy-start.1 = (f32[128,2048]{1,0:T(8,128)S(1)}, f32[128,2048]{1,0:T(8,128)}, u32[]{:S(2)}) copy-start(f32[128,2048]{1,0:T(8,128)} %reduce-scatter.3.cloned.1.call-done) | copy-start | bytes 3145732
  260.4 79.0 %all-gather.5.cloned.1.call-start = ((), (), s32[]{:S(2)}) async-start(), calls=%async_computation.7 | async-start | bytes 2621440 | tf_op jit(solution)/shard_map/all_gather | solution.py:61
  308.8 153.9 %all-reduce.5.cloned.1.call-start = ((), (), s32[]{:S(2)}) async-start(), calls=%async_computation.8 | async-start | bytes 8388608 | tf_op jit(solution)/shard_map/psum | solution.py:37
  462.7 3.6 copy-start.2
Sparse Core Ops, SparseCore 0:
  45.9 47.0 reduce-scatter.2
  95.3 30.4 all-gather.2
  136.5 112.5 all-reduce.2
  260.5 45.5 reduce-scatter.4
  308.9 30.4 all-gather.4
  350.1 112.5 all-reduce.4
where the time goes:
time: 507 us
  waiting for transfers between devices  379 us (75%)
  matrix products  49.6 us (10%)
  blocking collectives  41.2 us (8%)
  other arithmetic  19.9 us (4%)
  between operations  14.2 us (3%)
    psum x2, waiting for transfers between devices, residual_of(): summed = lax.psum(recon_part, 'atom')  225 us
    reduce_scatter x2, waiting for transfers between devices, body(): lax.psum_scatter(encode_rows(jnp.int32(0), lax.axis_size('dp') * row_coun...  92.9 us
    all_gather x2, waiting for transfers between devices, body(): lax.all_gather(sparse_codes.astype(jnp.bfloat16), 'dp', axis=0, tiled=True)  61 us
    dot_general x5, matrix products, product(): jnp.dot(left.astype(jnp.float32), right, precision=lax.Precision.HIGHEST,...  49.6 us
    all_to_all x1, blocking collectives, body(): lax.all_to_all(activations, 'dp', split_axis=1, concat_axis=0, tiled=True)  30.7 us
    convert_element_type x1, other arithmetic, body(): (updated * lax.rsqrt(squares / D + epsilon)).astype(jnp.bfloat16)  12.1 us
    psum x1, blocking collectives, body(): squares = lax.psum(jnp.sum(updated * updated, axis=0), 'dp')  10.5 us
  transfers between devices with their start and end apart: 6, of which 6 were waited for; matrix products, arithmetic and copies ran while one was open for 0% of the time, Pallas kernels for 0%

commit v1 on v0

--- a/solution.py
+++ b/solution.py
@@ -34,7 +34,9 @@
 
     def residual_of(coded_rows):
         recon_part = product(coded_rows, dict_wide.T)
-        summed = lax.psum(recon_part, "atom")
+        summed = recon_part
+        for hop in (1, 2, 4, 8, 16):
+            summed = summed + lax.ppermute(summed, "atom", [(dev, dev ^ hop) for dev in range(32)])
         full_residual = inputs - summed
         rounded = full_residual.astype(jnp.bfloat16)
         own_residual = lax.dynamic_slice_in_dim(full_residual, offset, share_rows, 0)

time: 507 us -> 1030 us (2.03)
  waiting for transfers between devices: 379 us -> 893 us
  starting transfers between devices: 0.43 us -> 15 us
  other arithmetic: 19.9 us -> 31.1 us
  matrix products: 49.6 us -> 39 us
    ppermute x0 -> x10, waiting for transfers between devices: none -> 737 us  [residual_of(): lax.ppermute(summed, 'atom', [(dev, dev ^ hop) for dev in range(32)])]
    psum x2 -> x0, waiting for transfers between devices: 225 us -> none  [residual_of(): summed = lax.psum(recon_part, 'atom')]
    ppermute x0 -> x10, starting transfers between devices: none -> 14.6 us  [residual_of(): lax.ppermute(summed, 'atom', [(dev, dev ^ hop) for dev in range(32)])]
    dot_general x5, matrix products: 49.6 us -> 39 us  [product(): jnp.dot(left.astype(jnp.float32), right, precision=lax.Precision.HIGHEST,...]
  transfers between devices with their start and end apart: 6 -> 14, of which waited for: 6 -> 14; matrix products, arithmetic and copies ran while one was open for 0% -> 0% of each run, Pallas kernels for 0% -> 0%
where the time goes in v1:
time: 1030 us
  waiting for transfers between devices  893 us (87%)
  blocking collectives  39.3 us (4%)
  matrix products  39 us (4%)
  other arithmetic  31.1 us (3%)
  starting transfers between devices  15 us (1%)
  between operations  13.9 us (1%)
    ppermute x10, waiting for transfers between devices, residual_of(): lax.ppermute(summed, 'atom', [(dev, dev ^ hop) for dev in range(32)])  737 us
    reduce_scatter x2, waiting for transfers between devices, body(): lax.psum_scatter(encode_rows(jnp.int32(0), lax.axis_size('dp') * row_coun...  93.9 us
    all_gather x2, waiting for transfers between devices, body(): lax.all_gather(sparse_codes.astype(jnp.bfloat16), 'dp', axis=0, tiled=True)  61.2 us
    dot_general x5, matrix products, product(): jnp.dot(left.astype(jnp.float32), right, precision=lax.Precision.HIGHEST,...  39 us
    all_to_all x1, blocking collectives, body(): lax.all_to_all(activations, 'dp', split_axis=1, concat_axis=0, tiled=True)  30.7 us
  transfers between devices with their start and end apart: 14, of which 14 were waited for; matrix products, arithmetic and copies ran while one was open for 0% of the time, Pallas kernels for 0%

profile of v1, /device:TPU:24, one launch (start us, length us, event | category | flops | bytes accessed | tf_op | source)
XLA Modules:
  0.0 1033.4 jit_solution(10804878712237008179)
XLA Ops:
  7.2 1.9 copy.8
  9.1 30.7 %all_to_all.19 = bf16[128,4,2048]{2,0,1:T(8,128)(2,1)S(1)} all-to-all(bf16[128,4,2048]{2,0,1:T(8,128)(2,1)S(1)} %bitcast.20), channel_id=1, replica_groups=mesh['atom'=32,'dp'=4] {'dp'}, dimensions={1} | all-to-all | bytes 4194304 | tf_op jit(solution)/shard_map/all_to_all | solution.py:30
  39.8 6.0 fusion.7
  45.8 0.0 all-gather.3.cloned.1.call-start
  45.9 47.2 %reduce-scatter.3.cloned.1.call-done = f32[128,2048]{1,0:T(8,128)} async-done(((f32[512,2048]{1,0:T(8,128)}), f32[128,2048]{1,0:T(8,128)}) %reduce-scatter.3.cloned.1.call-update) | async-done | bytes 1048592 | tf_op jit(solution)/shard_map/reduce_scatter | solution.py:56
  93.0 2.2 fusion.5
  95.2 0.0 reduce-scatter.5.cloned.1.call-start
  95.3 30.6 %all-gather.3.cloned.1.call-done = bf16[512,2048]{1,0:T(8,128)(2,1)} async-done(((bf16[128,2048]{1,0:T(8,128)(2,1)}), bf16[512,2048]{1,0:T(8,128)(2,1)}) %all-gather.3.cloned.1.call-update) | async-done | bytes 2097168 | tf_op jit(solution)/shard_map/all_gather | solution.py:63
  125.8 7.6 fusion.8
  133.5 0.1 collective-permute-start
  133.6 7.1 collective-permute-done
  140.7 0.8 add.51
  141.6 0.9 collective-permute-start.1
  142.5 91.8 %collective-permute-done.1 = f32[512,2048]{1,0:T(8,128)S(1)} collective-permute-done((f32[512,2048]{1,0:T(8,128)S(1)}, f32[512,2048]{1,0:T(8,128)S(1)}, u32[]{:S(2)}, u32[]{:S(2)}) %collective-permute-start.1) | collective-permute-done | bytes 4194336 | tf_op jit(solution)/shard_map/ppermute | solution.py:39
  234.2 0.8 add.52
  235.1 1.5 collective-permute-start.2
  236.6 91.8 %collective-permute-done.2 = f32[512,2048]{1,0:T(8,128)S(1)} collective-permute-done((f32[512,2048]{1,0:T(8,128)S(1)}, f32[512,2048]{1,0:T(8,128)S(1)}, u32[]{:S(2)}, u32[]{:S(2)}) %collective-permute-start.2) | collective-permute-done | bytes 4194336 | tf_op jit(solution)/shard_map/ppermute | solution.py:39
  328.4 1.1 add.53
  329.5 1.6 collective-permute-start.3
  331.2 89.3 %collective-permute-done.3 = f32[512,2048]{1,0:T(8,128)S(1)} collective-permute-done((f32[512,2048]{1,0:T(8,128)S(1)}, f32[512,2048]{1,0:T(8,128)S(1)}, u32[]{:S(2)}, u32[]{:S(2)}) %collective-permute-start.3) | collective-permute-done | bytes 4194336 | tf_op jit(solution)/shard_map/ppermute | solution.py:39
  420.5 1.1 add.54
  421.6 3.2 collective-permute-start.4
  424.8 88.4 %collective-permute-done.4 = f32[512,2048]{1,0:T(8,128)S(1)} collective-permute-done((f32[512,2048]{1,0:T(8,128)S(1)}, f32[512,2048]{1,0:T(8,128)S(1)}, u32[]{:S(2)}, u32[]{:S(2)}) %collective-permute-start.4) | collective-permute-done | bytes 4194336 | tf_op jit(solution)/shard_map/ppermute | solution.py:39
  513.2 6.3 fusion.1
  519.6 0.2 all-gather.5.cloned.1.call-start
  519.8 46.8 %reduce-scatter.5.cloned.1.call-done = f32[128,2048]{1,0:T(8,128)} async-done(((f32[512,2048]{1,0:T(8,128)}), f32[128,2048]{1,0:T(8,128)}) %reduce-scatter.5.cloned.1.call-update) | async-done | bytes 1048592 | tf_op jit(solution)/shard_map/reduce_scatter | solution.py:56
  566.6 2.6 fusion.6
  569.2 30.7 %all-gather.5.cloned.1.call-done = bf16[512,2048]{1,0:T(8,128)(2,1)} async-done(((bf16[128,2048]{1,0:T(8,128)(2,1)}), bf16[512,2048]{1,0:T(8,128)(2,1)}) %all-gather.5.cloned.1.call-update) | async-done | bytes 2097168 | tf_op jit(solution)/shard_map/all_gather | solution.py:63
  599.9 7.6 fusion.9
  607.5 0.1 collective-permute-start.5
  607.6 7.1 collective-permute-done.5
  614.8 0.8 add.57
  615.6 0.9 collective-permute-start.6
  616.5 91.8 %collective-permute-done.6 = f32[512,2048]{1,0:T(8,128)S(1)} collective-permute-done((f32[512,2048]{1,0:T(8,128)S(1)}, f32[512,2048]{1,0:T(8,128)S(1)}, u32[]{:S(2)}, u32[]{:S(2)}) %collective-permute-start.6) | collective-permute-done | bytes 4194336 | tf_op jit(solution)/shard_map/ppermute | solution.py:39
  708.3 1.1 add.58
  709.4 1.5 collective-permute-start.7
  710.9 91.8 %collective-permute-done.7 = f32[512,2048]{1,0:T(8,128)S(1)} collective-permute-done((f32[512,2048]{1,0:T(8,128)S(1)}, f32[512,2048]{1,0:T(8,128)S(1)}, u32[]{:S(2)}, u32[]{:S(2)}) %collective-permute-start.7) | collective-permute-done | bytes 4194336 | tf_op jit(solution)/shard_map/ppermute | solution.py:39
  802.7 1.1 add.59
  803.8 1.6 collective-permute-start.8
  805.4 89.4 %collective-permute-done.8 = f32[512,2048]{1,0:T(8,128)S(1)} collective-permute-done((f32[512,2048]{1,0:T(8,128)S(1)}, f32[512,2048]{1,0:T(8,128)S(1)}, u32[]{:S(2)}, u32[]{:S(2)}) %collective-permute-start.8) | collective-permute-done | bytes 4194336 | tf_op jit(solution)/shard_map/ppermute | solution.py:39
  894.8 2.8 add.60
  897.6 3.1 collective-permute-start.9
  900.7 88.7 %collective-permute-done.9 = f32[512,2048]{1,0:T(8,128)} collective-permute-done((f32[512,2048]{1,0:T(8,128)}, f32[512,2048]{1,0:T(8,128)}, u32[]{:S(2)}, u32[]{:S(2)}) %collective-permute-start.9) | collective-permute-done | bytes 4194336 | tf_op jit(solution)/shard_map/ppermute | solution.py:39
  989.4 4.6 convert_subtract_fusion
  994.0 0.7 constant_dynamic-slice_fusion
  994.7 11.4 %multiply_reduce_fusion = (f32[2048]{0:T(1024)S(1)}, f32[2048,2048]{1,0:T(8,128)}) fusion(bf16[2048,2048]{1,0:T(8,128)(2,1)} %param.3, bf16[512,2048]{1,0:T(8,128)(2,1)S(1)} %copy-done.2, f32[512,2048]{1,0:T(8,128)S(1)} %convert_subtract_fusion), kind=kOutput, calls=%fused_computation.1 | convolution fusion | flops 4316985344 | bytes 31465472 | tf_op jit(solution)/shard_map/dot_general | solution.py:19
  1006.1 8.6 psum.7
  1014.7 12.1 %multiply_convert_fusion = bf16[2048,2048]{1,0:T(8,128)(2,1)} fusion(f32[2048,2048]{1,0:T(8,128)} %get-tuple-element.6, bf16[2048,2048]{1,0:T(8,128)(2,1)} %param.3, f32[2048]{0:T(1024)S(1)} %add_rsqrt_fusion), kind=kLoop, calls=%fused_computation | loop fusion | flops 20971520 | bytes 33562624 | tf_op jit(solution)/shard_map/convert_element_type | solution.py:68
  (17 shorter events, 0.1 us)
Async XLA Ops:
  7.2 85.9 %reduce-scatter.3.cloned.1.call-start = ((), (), s32[]{:S(2)}) async-start(), calls=%async_computation.3 | async-start | bytes 5242880 | tf_op jit(solution)/shard_map/reduce_scatter | solution.py:56
  7.2 32.6 %copy-start = (bf16[2048,2048]{1,0:T(8,128)(2,1)S(1)}, bf16[2048,2048]{1,0:T(8,128)(2,1)}, u32[]{:S(2)}) copy-start(bf16[2048,2048]{1,0:T(8,128)(2,1)} %param.3) | copy-start | bytes 25165828
  45.8 80.0 %all-gather.3.cloned.1.call-start = ((), (), s32[]{:S(2)}) async-start(), calls=%async_computation.4 | async-start | bytes 2621440 | tf_op jit(solution)/shard_map/all_gather | solution.py:63
  95.2 471.4 %reduce-scatter.5.cloned.1.call-start = ((), (), s32[]{:S(2)}) async-start(), calls=%async_computation.5 | async-start | bytes 5242880 | tf_op jit(solution)/shard_map/reduce_scatter | solution.py:56
  133.5 7.2 collective-permute-start
  141.6 92.7 %collective-permute-start.1 = (f32[512,2048]{1,0:T(8,128)S(1)}, f32[512,2048]{1,0:T(8,128)S(1)}, u32[]{:S(2)}, u32[]{:S(2)}) collective-permute-start(f32[512,2048]{1,0:T(8,128)S(1)} %add.51), channel_id=1, source_target_pairs={{0,8},{4,12},{8,0},{12,4},{16,24},{20,28},{24,16},{28,20},{32,40},... | collective-permute-start | bytes 12582920 | tf_op jit(solution)/shard_map/ppermute | solution.py:39
  235.1 93.3 %collective-permute-start.2 = (f32[512,2048]{1,0:T(8,128)S(1)}, f32[512,2048]{1,0:T(8,128)S(1)}, u32[]{:S(2)}, u32[]{:S(2)}) collective-permute-start(f32[512,2048]{1,0:T(8,128)S(1)} %add.52), channel_id=1, source_target_pairs={{0,16},{4,20},{8,24},{12,28},{16,0},{20,4},{24,8},{28,12},{32,48},... | collective-permute-start | bytes 12582920 | tf_op jit(solution)/shard_map/ppermute | solution.py:39
  328.4 184.8 %slice-start = ((s8[8388608]{0:T(1024)(128)(4,1)}), s8[4194304]{0:T(1024)(128)(4,1)S(1)}, s32[]{:S(2)}) async-start(s8[8388608]{0:T(1024)(128)(4,1)} %bitcast.16), calls=%async_computation.7 | async-start | bytes 8388608
  329.5 183.7 %slice-start.1 = ((s8[8388608]{0:T(1024)(128)(4,1)}), s8[4194304]{0:T(1024)(128)(4,1)S(1)}, s32[]{:S(2)}) async-start(s8[8388608]{0:T(1024)(128)(4,1)} %bitcast.16), calls=%async_computation.8 | async-start | bytes 8388608
  329.5 91.0 %collective-permute-start.3 = (f32[512,2048]{1,0:T(8,128)S(1)}, f32[512,2048]{1,0:T(8,128)S(1)}, u32[]{:S(2)}, u32[]{:S(2)}) collective-permute-start(f32[512,2048]{1,0:T(8,128)S(1)} %add.53), channel_id=1, source_target_pairs={{0,32},{4,36},{8,40},{12,44},{16,48},{20,52},{24,56},{28,60},{32,0... | collective-permute-start | bytes 12582920 | tf_op jit(solution)/shard_map/ppermute | solution.py:39
  421.6 91.6 %collective-permute-start.4 = (f32[512,2048]{1,0:T(8,128)S(1)}, f32[512,2048]{1,0:T(8,128)S(1)}, u32[]{:S(2)}, u32[]{:S(2)}) collective-permute-start(f32[512,2048]{1,0:T(8,128)S(1)} %add.54), channel_id=1, source_target_pairs={{0,64},{4,68},{8,72},{12,76},{16,80},{20,84},{24,88},{28,92},{32,9... | collective-permute-start | bytes 12582920 | tf_op jit(solution)/shard_map/ppermute | solution.py:39
  519.6 47.0 %copy-start.1 = (f32[128,2048]{1,0:T(8,128)S(1)}, f32[128,2048]{1,0:T(8,128)}, u32[]{:S(2)}) copy-start(f32[128,2048]{1,0:T(8,128)} %reduce-scatter.3.cloned.1.call-done) | copy-start | bytes 3145732
  519.6 80.3 %all-gather.5.cloned.1.call-start = ((), (), s32[]{:S(2)}) async-start(), calls=%async_computation.6 | async-start | bytes 2621440 | tf_op jit(solution)/shard_map/all_gather | solution.py:63
  607.5 7.2 collective-permute-start.5
  615.6 92.7 %collective-permute-start.6 = (f32[512,2048]{1,0:T(8,128)S(1)}, f32[512,2048]{1,0:T(8,128)S(1)}, u32[]{:S(2)}, u32[]{:S(2)}) collective-permute-start(f32[512,2048]{1,0:T(8,128)S(1)} %add.57), channel_id=1, source_target_pairs={{0,8},{4,12},{8,0},{12,4},{16,24},{20,28},{24,16},{28,20},{32,40},... | collective-permute-start | bytes 12582920 | tf_op jit(solution)/shard_map/ppermute | solution.py:39
  709.4 93.3 %collective-permute-start.7 = (f32[512,2048]{1,0:T(8,128)S(1)}, f32[512,2048]{1,0:T(8,128)S(1)}, u32[]{:S(2)}, u32[]{:S(2)}) collective-permute-start(f32[512,2048]{1,0:T(8,128)S(1)} %add.58), channel_id=1, source_target_pairs={{0,16},{4,20},{8,24},{12,28},{16,0},{20,4},{24,8},{28,12},{32,48},... | collective-permute-start | bytes 12582920 | tf_op jit(solution)/shard_map/ppermute | solution.py:39
  803.8 91.0 %collective-permute-start.8 = (f32[512,2048]{1,0:T(8,128)S(1)}, f32[512,2048]{1,0:T(8,128)S(1)}, u32[]{:S(2)}, u32[]{:S(2)}) collective-permute-start(f32[512,2048]{1,0:T(8,128)S(1)} %add.59), channel_id=1, source_target_pairs={{0,32},{4,36},{8,40},{12,44},{16,48},{20,52},{24,56},{28,60},{32,0... | collective-permute-start | bytes 12582920 | tf_op jit(solution)/shard_map/ppermute | solution.py:39
  897.6 91.9 %collective-permute-start.9 = (f32[512,2048]{1,0:T(8,128)}, f32[512,2048]{1,0:T(8,128)}, u32[]{:S(2)}, u32[]{:S(2)}) collective-permute-start(f32[512,2048]{1,0:T(8,128)} %add.60), channel_id=1, source_target_pairs={{0,64},{4,68},{8,72},{12,76},{16,80},{20,84},{24,88},{28,92},{32,9... | collective-permute-start | bytes 12582920 | tf_op jit(solution)/shard_map/ppermute | solution.py:39
  900.7 94.0 %copy-start.2 = (bf16[512,2048]{1,0:T(8,128)(2,1)S(1)}, bf16[512,2048]{1,0:T(8,128)(2,1)}, u32[]{:S(2)}) copy-start(bf16[512,2048]{1,0:T(8,128)(2,1)} %all-gather.5.cloned.1.call-done) | copy-start | bytes 6291460
Sparse Core Ops, SparseCore 0:
  45.9 47.0 reduce-scatter.2
  95.3 30.4 all-gather.2
  519.7 46.8 reduce-scatter.4
  569.4 30.4 all-gather.4
